TPU v7x, 32 devices: a whole 2x2x4 slice. The times are simulated.
32 devices in a mesh: pipe: 8 (over z, core), tensor: 4 (over y, x).
Axes of the slice: x: 2, y: 2, z: 4, core: 2. Of those that a mesh axis runs over, the one named last changes fastest.
Arguments:
- held_rows: bfloat16 [8, 512, 2688], P('pipe', 'tensor'), may hold values from -6 to 6
- incoming: bfloat16 [1, 512, 2688], P(None, 'tensor'), may hold values from -6 to 6
- first_position: int32 [1], replicated, may hold values from 0 to 511
- in_gain: float32 [8, 2688], P('pipe'), may hold values from 0.5 to 1.5
- query_key_value_weight: bfloat16 [8, 2688, 16, 512], P('pipe', None, 'tensor'), may hold values from -0.125 to 0.125
- q_gain: float32 [8, 128], P('pipe'), may hold values from 0.5 to 1.5
- k_gain: float32 [8, 128], P('pipe'), may hold values from 0.5 to 1.5
- cached_key_rows: bfloat16 [8, 16, 1024, 128], P('pipe', 'tensor'), may hold values from -3 to 3
- cached_value_rows: bfloat16 [8, 16, 1024, 128], P('pipe', 'tensor'), may hold values from -6 to 6
- w_out: bfloat16 [8, 4096, 2688], P('pipe', 'tensor'), may hold values from -0.09375 to 0.09375
- post_gain: float32 [8, 2688], P('pipe'), may hold values from 0.5 to 1.5
Outputs:
- hidden: bfloat16 [8, 2, 512, 2688], P('pipe', None, 'tensor')
All inputs are finite; a program needn't handle non-finite values.
Results may differ from a plain program's by a relative error of at most 0.015.
Values may be sent and summed in bfloat16 or wider, within the bound.
No kernel may reach another device: no remote copies, remote signals or barrier semaphores. Data moves between devices by JAX's collectives and lax.ppermute only.
A program may use at most 128 MiB of HBM per device.

v0:
```python
import math
import jax
import jax.numpy as jnp
from jax import lax
from jax.sharding import PartitionSpec as P

HEAD_SIZE = 128
WINDOW_LENGTH = 1024
TICKS = 2
ROWS = 512
query_scale = 168.0 ** (-0.5)
norm_eps = 1e-06
rope_base = 10000.0


def shifted(block, axis, distance):
    devices = range(lax.axis_size(axis))
    route = [(i - distance, i) for i in devices if i - distance in devices]
    return lax.ppermute(block, axis, route)


def rms_scale(values, gain_vec):
    mean_square = jnp.mean(values * values, axis=-1, keepdims=True)
    return values * lax.rsqrt(mean_square + norm_eps) * gain_vec


def rotate(values, positions):
    half_width = values.shape[-1] // 2
    frequency = jnp.exp(
        jnp.arange(half_width, dtype=jnp.float32) * (-math.log(rope_base) / half_width)
    )
    angles = positions.astype(jnp.float32)[:, None] * frequency[None, :]
    angles = angles.reshape((angles.shape[0],) + (1,) * (values.ndim - 2) + (half_width,))
    cosine = jnp.cos(angles)
    sine_part = jnp.sin(angles)
    first_half = values[..., :half_width]
    second = values[..., half_width:]
    return jnp.concatenate(
        [first_half * cosine - second * sine_part, second * cosine + first_half * sine_part],
        axis=-1,
    )


def attend(projected_rows, prev_keys, prev_values, start_pos, q_scale, k_scale):
    row_total = projected_rows.shape[0]
    kv_local = prev_keys.shape[0]
    group_size = projected_rows.shape[1] // (kv_local * HEAD_SIZE) - 2
    blocks = projected_rows.reshape(row_total, kv_local, group_size + 2, HEAD_SIZE)
    query_pos = start_pos + jnp.arange(row_total, dtype=jnp.int32)
    queries = rotate(rms_scale(blocks[:, :, :group_size], q_scale), query_pos).astype(jnp.bfloat16)
    key_rows = rotate(rms_scale(blocks[:, :, group_size], k_scale), query_pos).astype(jnp.bfloat16)
    value_rows = blocks[:, :, group_size + 1].astype(jnp.bfloat16)
    key_heads = jnp.swapaxes(key_rows, 0, 1)
    value_heads = jnp.swapaxes(value_rows, 0, 1)
    all_keys = jnp.concatenate([prev_keys, key_heads], axis=1)
    all_values = jnp.concatenate([prev_values, value_heads], axis=1)
    prev_length = prev_keys.shape[1]
    key_pos = start_pos - prev_length + jnp.arange(prev_length + row_total, dtype=jnp.int32)
    visible = (
        (key_pos[None, :] <= query_pos[:, None])
        & (key_pos[None, :] > query_pos[:, None] - WINDOW_LENGTH)
        & (key_pos[None, :] >= 0)
    )
    scores = (
        jnp.einsum("rkgd,kld->kgrl", queries, all_keys, preferred_element_type=jnp.float32)
        * query_scale
    )
    weights = jnp.where(visible[None, None], jnp.exp(scores), 0.0)
    totals = jnp.sum(weights, axis=-1, keepdims=True)
    mixed_heads = (
        jnp.einsum(
            "kgrl,kld->kgrd",
            weights.astype(jnp.bfloat16),
            all_values,
            preferred_element_type=jnp.float32,
        )
        / totals
    )
    mixed_heads = jnp.transpose(mixed_heads.astype(jnp.bfloat16), (2, 0, 1, 3)).reshape(
        row_total, -1
    )
    return (mixed_heads, key_heads, value_heads)


def shards(
    held_rows,
    incoming,
    first_position,
    in_gain,
    query_key_value_weight,
    q_gain,
    k_gain,
    cached_key_rows,
    cached_value_rows,
    w_out,
    post_gain,
):
    section_id = lax.axis_index("pipe")
    section_count = lax.axis_size("pipe")
    model_width = held_rows.shape[2]
    in_scale = in_gain[0]
    post_scale = post_gain[0]
    q_scale = q_gain[0]
    k_scale = k_gain[0]
    w_flat = query_key_value_weight[0].reshape(model_width, -1)
    w_local = w_out[0]
    prev_keys = cached_key_rows[0]
    prev_values = cached_value_rows[0]
    outputs = []
    current = held_rows[0]
    for micro_step in range(TICKS):
        start_pos = first_position[0] + (section_count - 1 - section_id + micro_step) * ROWS
        projected_rows = jnp.dot(
            (
                lax.all_gather(current, "tensor", axis=0, tiled=True).astype(jnp.float32) * in_scale
            ).astype(jnp.bfloat16),
            w_flat,
            preferred_element_type=jnp.float32,
        )
        mixed_heads, key_heads, value_heads = attend(
            projected_rows, prev_keys, prev_values, start_pos, q_scale, k_scale
        )
        summed = lax.psum_scatter(
            jnp.dot(mixed_heads, w_local, preferred_element_type=jnp.float32).astype(jnp.bfloat16),
            "tensor",
            scatter_dimension=0,
            tiled=True,
        ).astype(jnp.float32)
        hidden = (current.astype(jnp.float32) + rms_scale(summed, post_scale)).astype(jnp.bfloat16)
        outputs.append(hidden)
        if micro_step + 1 < TICKS:
            prev_keys = jnp.concatenate([prev_keys, key_heads], axis=1)
            prev_values = jnp.concatenate([prev_values, value_heads], axis=1)
            passed = shifted(hidden, "pipe", 1)
            current = jnp.where(section_id == 0, incoming[micro_step], passed)
    return jnp.stack(outputs, axis=0)[None]


def solution(mesh):
    return jax.shard_map(
        shards,
        mesh=mesh,
        in_specs=(
            P("pipe", "tensor", None),
            P(None, "tensor", None),
            P(),
            P("pipe", None),
            P("pipe", None, "tensor", None),
            P("pipe", None),
            P("pipe", None),
            P("pipe", "tensor", None, None),
            P("pipe", "tensor", None, None),
            P("pipe", "tensor", None),
            P("pipe", None),
        ),
        out_specs=P("pipe", None, "tensor", None),
        check_vma=False,
    )
```

profile of v0, /device:TPU:0, one launch (start us, length us, event | category | flops | bytes accessed | tf_op | source)
XLA Modules:
  0.0 297.5 jit_solution(13383296722176563755)
XLA Ops:
  6.5 0.0 all-gather.6.cloned.1.call-start
  6.5 0.7 all-gather.6.cloned.1.call-update
  7.3 0.0 reduce-scatter.3.cloned.1.call-start
  8.0 1.5 copy.15
  9.4 12.3 %copy.35 = bf16[336,8,4,512]{3,1,2,0:T(8,128)(2,1)} copy(bf16[336,8,4,512]{3,2,1,0:T(4,128)(2,1)} %bitcast.133) | data formatting | bytes 22020096
  21.7 14.2 %copy.12 = bf16[2048,2688]{1,0:T(8,128)(2,1)} copy(bf16[2048,2688]{0,1:T(8,128)(2,1)} %bitcast.132) | data formatting | bytes 22020096 | tf_op jit(solution)/shard_map/dot_general | solution.py:113
  35.9 0.0 copy-done.7
  36.0 1.0 multiply_cosine_fusion
  37.0 1.1 and_and_fusion.1
  38.1 14.4 %all-gather.6.cloned.1.call-done = bf16[1,512,2688]{2,1,0:T(8,128)(2,1)} async-done(((bf16[1,128,2688]{2,1,0:T(8,128)(2,1)}), bf16[1,512,2688]{2,1,0:T(8,128)(2,1)}) %all-gather.6.cloned.1.call-update) | async-done | bytes 2752528 | tf_op jit(solution)/shard_map/all_gather | solution.py:115
  52.5 9.8 %fusion.27 = f32[512,4,4,128]{0,3,2,1:T(8,128)S(1)} fusion(bf16[4,4,128,2688]{3,2,1,0:T(8,128)(2,1)} %bitcast.134, bf16[1,512,2688]{2,1,0:T(8,128)(2,1)} %all-gather.6.cloned.1.call-done, f32[2688]{0:T(1024)S(1)} %reduce), kind=kOutput, calls=%fused_computation.26 | convolution fusion | flops 5641273344 | bytes 17967616 | tf_op jit(solution)/shard_map/dot_general | solution.py:113
  62.3 0.0 copy-start.9
  62.3 0.0 copy-start.10
  62.3 0.1 multiply_reduce_fusion.3
  62.5 0.3 multiply_reduce_fusion.1
  62.7 0.9 fusion.67
  63.7 0.0 copy-done.9
  63.7 0.2 multiply_multiply_fusion.3
  63.9 0.0 copy-done.10
  63.9 0.5 multiply_multiply_fusion.1
  64.4 1.3 subtract_convert_fusion.1
  65.7 0.2 subtract_convert_fusion.3
  65.9 0.3 copy.13
  66.2 0.0 copy-start.5
  66.2 0.0 copy-start.3
  66.2 0.0 slice-start
  66.2 12.5 %fusion.2 = (f32[4,2,512]{2,1,0:T(2,128)S(1)}, f32[4,1536,512,2]{2,1,3,0:T(8,128)}) fusion(pred[512,1536]{0,1:T(8,128)(4,1)S(1)} %and_and_fusion.1, bf16[512,4,2,64]{0,3,2,1:T(8,128)(2,1)} %get-tuple-element.8, bf16[512,4,2,64]{0,3,2,1:T(8,128)(2,1)} %get-tuple-element.7, bf16[4,512,128]{2,1,0:T(8,128)(2,1)S(1)} %copy.13, bf16[4,1024,128]{2,1,0:T(8,128)(2,1)} %bitcast.145), kind=kOutput, calls=%fused_computation.4 | convolution fusion | flops 1634725888 | bytes 28590080 | tf_op jit(solution)/shard_map/rkgd,kld->kgrl/dot_general | solution.py:65
  78.7 0.0 copy-done.5
  78.8 0.0 slice-start.1
  78.8 11.2 %fusion.42 = bf16[512,4,2,128]{0,3,2,1:T(8,128)(2,1)S(1)} fusion(f32[4,1536,512,2]{2,1,3,0:T(8,128)} %get-tuple-element.20, pred[512,1536]{0,1:T(8,128)(4,1)S(1)} %and_and_fusion.1, bf16[4,512,128]{1,2,0:T(8,128)(2,1)S(1)} %copy-done.3, bf16[4,1024,128]{1,2,0:T(8,128)(2,1)S(1)} %bitcast.137, f32[512,4,2]{0,2,1:T(2,128)S(1)} %bitcast.150), kind=kOutput, calls=%fused_computation.44 | convolution fusion | flops 1633681408 | bytes 28590080 | tf_op jit(solution)/shard_map/kgrl,kld->kgrd/dot_general | solution.py:71
  90.0 0.0 slice-done
  90.0 0.0 slice-done.1
  90.0 0.0 copy-start.8
  90.0 4.5 %fusion.17 = bf16[512,2688]{1,0:T(8,128)(2,1)} fusion(bf16[512,1024]{0,1:T(8,128)(2,1)S(1)} %bitcast.148, bf16[1,1024,2688]{2,1,0:T(8,128)(2,1)S(1)} %bitcast.144), kind=kOutput, calls=%fused_computation.19 | convolution fusion | flops 2819948544 | bytes 9306112 | tf_op jit(solution)/shard_map/dot_general | solution.py:124
  94.5 0.0 reduce-scatter.3.cloned.1.call-update
  94.6 0.0 all-gather.4.cloned.1.call-start
  94.6 40.7 %reduce-scatter.3.cloned.1.call-done = bf16[128,2688]{1,0:T(8,128)(2,1)} async-done(((bf16[512,2688]{1,0:T(8,128)(2,1)}), bf16[128,2688]{1,0:T(8,128)(2,1)}) %reduce-scatter.3.cloned.1.call-update) | async-done | bytes 688144 | tf_op jit(solution)/shard_map/reduce_scatter | solution.py:123
  135.3 1.3 fusion.52
  136.7 1.4 fusion.55
  138.1 1.6 collective-permute-start
  139.7 1.7 collective-permute-done
  141.4 0.9 bitcast_select_fusion.2
  142.3 0.0 all-gather.4.cloned.1.call-update
  142.4 0.0 reduce-scatter.5.cloned.1.call-start
  142.5 2.5 and_and_fusion
  145.0 47.1 %all-gather.4.cloned.1.call-done = bf16[512,2688]{1,0:T(8,128)(2,1)} async-done(((bf16[128,2688]{1,0:T(8,128)(2,1)}), bf16[512,2688]{1,0:T(8,128)(2,1)}) %all-gather.4.cloned.1.call-update) | async-done | bytes 2752528 | tf_op jit(solution)/shard_map/all_gather | solution.py:115
  192.0 9.8 %fusion.24 = f32[512,4,4,128]{0,3,2,1:T(8,128)S(1)} fusion(bf16[4,4,128,2688]{3,2,1,0:T(8,128)(2,1)} %bitcast.135, bf16[512,2688]{1,0:T(8,128)(2,1)} %all-gather.4.cloned.1.call-done, f32[2688]{0:T(1024)S(1)} %reduce), kind=kOutput, calls=%fused_computation.24 | convolution fusion | flops 5641273344 | bytes 17967616 | tf_op jit(solution)/shard_map/dot_general | solution.py:113
  201.8 0.1 multiply_reduce_fusion.2
  201.9 0.3 multiply_reduce_fusion
  202.2 0.9 fusion.68
  203.1 0.1 multiply_multiply_fusion.2
  203.3 0.5 multiply_multiply_fusion
  203.8 1.4 subtract_convert_fusion
  205.1 0.2 subtract_convert_fusion.2
  205.4 1.0 copy.19
  206.4 17.0 %fusion = (f32[4,2,512]{2,1,0:T(2,128)S(1)}, f32[4,2048,512,2]{2,1,3,0:T(8,128)}) fusion(pred[512,2048]{0,1:T(8,128)(4,1)} %and_and_fusion, bf16[512,4,2,64]{0,3,2,1:T(8,128)(2,1)} %get-tuple-element.6, bf16[512,4,2,64]{0,3,2,1:T(8,128)(2,1)} %get-tuple-element.5, bf16[4,512,128]{2,1,0:T(8,128)(2,1)} %copy.19, bf16[4,512,128]{2,1,0:T(8,128)(2,1)S(1)} %copy-done.6, ...), kind=kOutput, calls=%fused_computation.1 | convolution fusion | flops 2181033984 | bytes 37765120 | tf_op jit(solution)/shard_map/rkgd,kld->kgrl/dot_general | solution.py:65
  223.3 0.0 copy-done.4
  223.3 15.1 %fusion.41 = bf16[512,4,2,128]{0,3,2,1:T(8,128)(2,1)} fusion(f32[4,2048,512,2]{2,1,3,0:T(8,128)} %get-tuple-element.22, pred[512,2048]{0,1:T(8,128)(4,1)} %and_and_fusion, bf16[4,512,128]{1,2,0:T(8,128)(2,1)} %fusion.68, bf16[4,512,128]{1,2,0:T(8,128)(2,1)S(1)} %copy-done.4, bf16[4,1024,128]{1,2,0:T(8,128)(2,1)S(1)} %bitcast.138, f32[512,4,2]{0,2,1:T(2,128)S(1)} %bitcast.149), kind=kOutput, calls=%fused_computation.42 | convolution fusion | flops 2179989504 | bytes 37765120 | tf_op jit(solution)/shard_map/kgrl,kld->kgrd/dot_general | solution.py:71
  238.5 7.7 %fusion.20 = bf16[512,2688]{1,0:T(8,128)(2,1)} fusion(bf16[512,1024]{0,1:T(8,128)(2,1)} %bitcast.147, bf16[1,1024,2688]{2,1,0:T(8,128)(2,1)} %param.20), kind=kOutput, calls=%fused_computation.20 | convolution fusion | flops 2819948544 | bytes 9306112 | tf_op jit(solution)/shard_map/dot_general | solution.py:124
  246.1 0.0 reduce-scatter.5.cloned.1.call-update
  246.1 40.8 %reduce-scatter.5.cloned.1.call-done = bf16[128,2688]{1,0:T(8,128)(2,1)} async-done(((bf16[512,2688]{1,0:T(8,128)(2,1)}), bf16[128,2688]{1,0:T(8,128)(2,1)}) %reduce-scatter.5.cloned.1.call-update) | async-done | bytes 688144 | tf_op jit(solution)/shard_map/reduce_scatter | solution.py:123
  286.9 1.3 fusion.56
  288.3 1.4 fusion.66
  289.7 1.2 maximum_bitcast_fusion.10
  (31 shorter events, 0.3 us)
Async XLA Ops:
  6.5 46.0 %all-gather.6.cloned.1.call-start = ((), (), s32[]{:S(2)}) async-start(), calls=%async_computation.5 | async-start | bytes 3440640 | tf_op jit(solution)/shard_map/all_gather | solution.py:115
  7.3 128.1 %reduce-scatter.3.cloned.1.call-start = ((), (), s32[]{:S(2)}) async-start(), calls=%async_computation.2 | async-start | bytes 3440640 | tf_op jit(solution)/shard_map/reduce_scatter | solution.py:123
  21.7 14.2 %copy-start.7 = (f32[1,2688]{1,0:T(1,128)S(1)}, f32[1,2688]{1,0:T(1,128)}, u32[]{:S(2)}) copy-start(f32[1,2688]{1,0:T(1,128)} %param.14) | copy-start | bytes 32260
  62.3 1.4 copy-start.9
  62.3 1.6 copy-start.10
  66.2 12.5 %copy-start.5 = (bf16[4,512,128]{2,1,0:T(8,128)(2,1)}, bf16[4,512,128]{2,1,0:T(8,128)(2,1)S(1)}, u32[]{:S(2)}) copy-start(bf16[4,512,128]{2,1,0:T(8,128)(2,1)S(1)} %copy.13) | copy-start | bytes 1572868
  66.2 12.5 %copy-start.3 = (bf16[4,512,128]{1,2,0:T(8,128)(2,1)S(1)}, bf16[4,512,128]{1,2,0:T(8,128)(2,1)}, u32[]{:S(2)}) copy-start(bf16[4,512,128]{1,2,0:T(8,128)(2,1)} %fusion.67) | copy-start | bytes 1572868
  66.2 23.7 %slice-start = ((s8[5505024]{0:T(1024)(128)(4,1)}), s8[4194304]{0:T(1024)(128)(4,1)S(1)}, s32[]{:S(2)}) async-start(s8[5505024]{0:T(1024)(128)(4,1)} %bitcast.143), calls=%async_computation.6 | async-start | bytes 8388608
  78.8 11.2 %slice-start.1 = ((s8[5505024]{0:T(1024)(128)(4,1)}), s8[1310720]{0:T(1024)(128)(4,1)S(1)}, s32[]{:S(2)}) async-start(s8[5505024]{0:T(1024)(128)(4,1)} %bitcast.143), calls=%async_computation.7 | async-start | bytes 2621440
  90.0 4.6 %copy-start.8 = (f32[1,2688]{1,0:T(1,128)S(1)}, f32[1,2688]{1,0:T(1,128)}, u32[]{:S(2)}) copy-start(f32[1,2688]{1,0:T(1,128)} %param.21) | copy-start | bytes 32260
  94.5 42.2 %copy-start.1 = (bf16[1,128,2688]{2,1,0:T(8,128)(2,1)S(1)}, bf16[1,128,2688]{2,1,0:T(8,128)(2,1)}, u32[]{:S(2)}) copy-start(bf16[1,128,2688]{2,1,0:T(8,128)(2,1)} %param.11) | copy-start | bytes 2064388
  94.5 46.9 %copy-start.2 = (bf16[1,128,2688]{2,1,0:T(8,128)(2,1)S(1)}, bf16[1,128,2688]{2,1,0:T(8,128)(2,1)}, u32[]{:S(2)}) copy-start(bf16[1,128,2688]{2,1,0:T(8,128)(2,1)} %param.12) | copy-start | bytes 2064388
  94.6 97.5 %all-gather.4.cloned.1.call-start = ((), (), s32[]{:S(2)}) async-start(), calls=%async_computation.3 | async-start | bytes 3440640 | tf_op jit(solution)/shard_map/all_gather | solution.py:115
  138.1 3.3 %collective-permute-start = (bf16[128,2688]{1,0:T(8,128)(2,1)S(1)}, bf16[128,2688]{1,0:T(8,128)(2,1)S(1)}, u32[]{:S(2)}, u32[]{:S(2)}) collective-permute-start(bf16[128,2688]{1,0:T(8,128)(2,1)S(1)} %fusion.55), channel_id=1, source_target_pairs={{0,4},{4,8},{8,12},{12,16},{16,20},{20,24},{24,28},{1,5},{5,9},{9,... | collective-permute-start | bytes 2064392 | tf_op jit(solution)/shard_map/ppermute | solution.py:19
  142.4 144.6 %reduce-scatter.5.cloned.1.call-start = ((), (), s32[]{:S(2)}) async-start(), calls=%async_computation.4 | async-start | bytes 3440640 | tf_op jit(solution)/shard_map/reduce_scatter | solution.py:123
  203.8 2.6 copy-start.6
  206.4 17.0 %copy-start.4 = (bf16[4,512,128]{1,2,0:T(8,128)(2,1)S(1)}, bf16[4,512,128]{1,2,0:T(8,128)(2,1)}, u32[]{:S(2)}) copy-start(bf16[4,512,128]{1,2,0:T(8,128)(2,1)} %fusion.67) | copy-start | bytes 1572868
  246.1 42.2 %copy-start = (bf16[128,2688]{1,0:T(8,128)(2,1)S(1)}, bf16[128,2688]{1,0:T(8,128)(2,1)}, u32[]{:S(2)}) copy-start(bf16[128,2688]{1,0:T(8,128)(2,1)} %bitcast_select_fusion.2) | copy-start | bytes 2064388
Sparse Core Ops, SparseCore 0:
  9.2 43.3 all-gather.5
  94.7 40.6 reduce-scatter.2
  142.5 49.5 all-gather.3
  246.3 40.6 reduce-scatter.4
where the time goes:
time: 298 us; the launch traced here: 297 us
  waiting for transfers between devices  145 us (49%)
  matrix products  87.5 us (29%)
  local copies, waits for them, and re-layouts  31.1 us (10%)
  other arithmetic  17.6 us (6%)
  between operations  14.2 us (5%)
    reduce_scatter x2, waiting for transfers between devices, shards(): lax.psum_scatter(jnp.dot(mixed_heads, w_local, preferred_element_type=jnp...  81.5 us
    all_gather x2, waiting for transfers between devices, shards(): lax.all_gather(current, 'tensor', axis=0, tiled=True).astype(jnp.float32)  61.5 us
    dot_general x2, matrix products, attend(): jnp.einsum('rkgd,kld->kgrl', queries, all_keys, preferred_element_type=jn...  29.5 us
    dot_general x2, matrix products, attend(): jnp.einsum('kgrl,kld->kgrd', weights.astype(jnp.bfloat16), all_values, pr...  26.3 us
    dot_general x2, matrix products, shards(): jnp.dot((lax.all_gather(current, 'tensor', axis=0, tiled=True).astype(jnp...  19.5 us
    dot_general x1, local copies, waits for them, and re-layouts, shards(): jnp.dot((lax.all_gather(current, 'tensor', axis=0, tiled=True).astype(jnp...  14.2 us
    unnamed x28, local copies, waits for them, and re-layouts  13.8 us
    dot_general x2, matrix products, shards(): jnp.dot(mixed_heads, w_local, preferred_element_type=jnp.float32)  12.2 us
  transfers between devices with their start and end apart: 5, of which 5 were waited for; matrix products, arithmetic and copies ran while one was open for 11% of the time, Pallas kernels for 0%

commit v1 on v0

--- a/solution.py
+++ b/solution.py
@@ -3,6 +3,7 @@
 import jax.numpy as jnp
 from jax import lax
 from jax.sharding import PartitionSpec as P
+from jax.lax import axis_index, axis_size, ppermute
 
 HEAD_SIZE = 128
 WINDOW_LENGTH = 1024
@@ -11,6 +12,12 @@
 query_scale = 168.0 ** (-0.5)
 norm_eps = 1e-06
 rope_base = 10000.0
+
+
+def feed_the_scales(x_in, d_out):
+    x_in = jnp.moveaxis(x_in, 0, d_out)
+    u1 = x_in.shape
+    return x_in.reshape(*u1[:d_out], u1[d_out] * u1[d_out + 1], *u1[d_out + 2 :])
 
 
 def shifted(block, axis, distance):
@@ -110,10 +117,30 @@
     current = held_rows[0]
     for micro_step in range(TICKS):
         start_pos = first_position[0] + (section_count - 1 - section_id + micro_step) * ROWS
+
+        def outputs_plan(inner_x, group_axis, dim_i):
+            slots = axis_size(group_axis)
+            line_up = [(ix, (ix + 1) % slots) for ix in range(slots)]
+            blocks_here = [(idx, at) for at, idx in line_up]
+            piece_next, arr_now = ([], [])
+            for t in range(slots - 1):
+                if t % 2 == 0:
+                    front = ppermute(piece_next[-1] if piece_next else inner_x, group_axis, line_up)
+                    piece_next.append(front)
+                else:
+                    w2 = ppermute(arr_now[-1] if arr_now else inner_x, group_axis, blocks_here)
+                    arr_now.append(w2)
+            tile_out = jnp.stack([*piece_next[::-1], inner_x, *arr_now])
+            formed = axis_index(group_axis)
+            seen_now = len(piece_next)
+            low = formed - seen_now
+            tile_out = tile_out[(jnp.arange(slots) - low) % slots]
+            return feed_the_scales(tile_out, dim_i)
+
         projected_rows = jnp.dot(
-            (
-                lax.all_gather(current, "tensor", axis=0, tiled=True).astype(jnp.float32) * in_scale
-            ).astype(jnp.bfloat16),
+            (outputs_plan(current, "tensor", 0).astype(jnp.float32) * in_scale).astype(
+                jnp.bfloat16
+            ),
             w_flat,
             preferred_element_type=jnp.float32,
         )

time: 298 us -> 320 us (1.074)
  starting transfers between devices: 1.74 us -> 10.4 us
  other arithmetic: 17.6 us -> 25.8 us
  local copies, waits for them, and re-layouts: 31.1 us -> 37.5 us
    all_gather x2 -> x0, waiting for transfers between devices: 61.5 us -> none  [shards(): lax.all_gather(current, 'tensor', axis=0, tiled=True).astype(jnp.float32)]
    ppermute x0 -> x6, waiting for transfers between devices: none -> 48.7 us  [the longest x4 37.1 us: outputs_plan(): ppermute(piece_next[-1] if piece_next else inner_x, group_axis, line_up)]
    reduce_scatter x2, waiting for transfers between devices: 81.5 us -> 94.6 us  [shards(): lax.psum_scatter(jnp.dot(mixed_heads, w_local, preferred_element_type=jnp...]
    ppermute x0 -> x6, starting transfers between devices: none -> 8.77 us  [the longest x4 6.34 us: outputs_plan(): ppermute(piece_next[-1] if piece_next else inner_x, group_axis, line_up)]
    gather x0 -> x2, local copies, waits for them, and re-layouts: none -> 4.72 us  [outputs_plan(): tile_out = tile_out[(jnp.arange(slots) - low) % slots]]
    convert_element_type x1 -> x2, other arithmetic: 0.01 us -> 4.45 us  [shards(): (outputs_plan(current, 'tensor', 0).astype(jnp.float32) * in_scale).astyp...]
    unnamed x28 -> x50, local copies, waits for them, and re-layouts: 13.8 us -> 16.5 us
  transfers between devices with their start and end apart: 5 -> 9, of which waited for: 5 -> 7; matrix products, arithmetic and copies ran while one was open for 11% -> 11% of each run, Pallas kernels for 0% -> 0%
where the time goes in v1:
time: 320 us; the launch traced here: 319 us
  waiting for transfers between devices  145 us (45%)
  matrix products  85.6 us (27%)
  local copies, waits for them, and re-layouts  37.5 us (12%)
  other arithmetic  25.8 us (8%)
  between operations  14.5 us (5%)
  starting transfers between devices  10.4 us (3%)
    reduce_scatter x2, waiting for transfers between devices, shards(): lax.psum_scatter(jnp.dot(mixed_heads, w_local, preferred_element_type=jnp...  94.6 us
    ppermute x4, waiting for transfers between devices, outputs_plan(): ppermute(piece_next[-1] if piece_next else inner_x, group_axis, line_up)  37.1 us
    dot_general x2, matrix products, attend(): jnp.einsum('rkgd,kld->kgrl', queries, all_keys, preferred_element_type=jn...  29.2 us
    dot_general x2, matrix products, attend(): jnp.einsum('kgrl,kld->kgrd', weights.astype(jnp.bfloat16), all_values, pr...  26.1 us
    dot_general x2, matrix products, shards(): jnp.dot((outputs_plan(current, 'tensor', 0).astype(jnp.float32) * in_scal...  17.9 us
    unnamed x50, local copies, waits for them, and re-layouts  16.5 us
    dot_general x1, local copies, waits for them, and re-layouts, shards(): jnp.dot((outputs_plan(current, 'tensor', 0).astype(jnp.float32) * in_scal...  14.1 us
    dot_general x2, matrix products, shards(): jnp.dot(mixed_heads, w_local, preferred_element_type=jnp.float32)  12.3 us
  transfers between devices with their start and end apart: 9, of which 7 were waited for; matrix products, arithmetic and copies ran while one was open for 11% of the time, Pallas kernels for 0%

profile of v1, /device:TPU:0, one launch (start us, length us, event | category | flops | bytes accessed | tf_op | source)
XLA Modules:
  0.0 318.8 jit_solution(2927062476415241471)
XLA Ops:
  6.5 3.0 collective-permute-start
  9.5 1.0 collective-permute-start.2
  11.1 2.3 copy.15
  13.5 12.1 %copy.35 = bf16[336,8,4,512]{3,1,2,0:T(8,128)(2,1)} copy(bf16[336,8,4,512]{3,2,1,0:T(4,128)(2,1)} %bitcast.137) | data formatting | bytes 22020096
  25.5 14.1 %copy.12 = bf16[2048,2688]{1,0:T(8,128)(2,1)} copy(bf16[2048,2688]{0,1:T(8,128)(2,1)} %bitcast.136) | data formatting | bytes 22020096 | tf_op jit(solution)/shard_map/dot_general | solution.py:140
  39.8 1.3 collective-permute-start.1
  41.1 1.8 multiply_cosine_fusion
  42.8 1.8 and_and_fusion.1
  44.7 13.1 %collective-permute-done.1 = bf16[128,2688]{1,0:T(8,128)(2,1)S(1)} collective-permute-done((bf16[128,2688]{1,0:T(8,128)(2,1)S(1)}, bf16[128,2688]{1,0:T(8,128)(2,1)S(1)}, u32[]{:S(2)}, u32[]{:S(2)}) %collective-permute-start.1) | collective-permute-done | bytes 688160 | tf_op jit(solution)/shard_map/ppermute | solution.py:128
  57.8 1.5 pad_maximum_fusion
  59.4 2.4 gather_fusion
  61.7 2.2 multiply_convert_fusion.1
  64.0 8.9 %fusion.73 = f32[512,4,4,128]{0,3,2,1:T(8,128)S(1)} fusion(bf16[512,2688,1,1]{1,0,3,2:T(8,128)(2,1)S(1)} %bitcast.142, bf16[4,4,128,2688]{3,2,1,0:T(8,128)(2,1)} %bitcast.138), kind=kOutput, calls=%fused_computation.129 | convolution fusion | flops 5637144576 | bytes 17956864 | tf_op jit(solution)/shard_map/dot_general | solution.py:140
  72.9 0.1 multiply_reduce_fusion.3
  73.1 0.3 multiply_reduce_fusion.1
  73.3 0.1 fusion.57
  73.5 0.1 copy-done.20
  73.6 0.2 multiply_multiply_fusion.3
  73.8 0.5 multiply_multiply_fusion.1
  74.3 0.3 copy-done.5
  74.5 0.1 copy-done.6
  74.6 1.3 subtract_convert_fusion.1
  75.9 0.2 subtract_convert_fusion.3
  76.1 0.3 copy.13
  76.4 0.6 copy-done.10
  77.1 12.4 %fusion.2 = (f32[4,2,512]{2,1,0:T(2,128)S(1)}, f32[4,1536,512,2]{2,1,3,0:T(8,128)}) fusion(pred[512,1536]{0,1:T(8,128)(4,1)S(1)} %copy-done.10, bf16[512,4,2,64]{0,3,2,1:T(8,128)(2,1)} %get-tuple-element.8, bf16[512,4,2,64]{0,3,2,1:T(8,128)(2,1)} %get-tuple-element.7, bf16[4,512,128]{2,1,0:T(8,128)(2,1)S(1)} %copy.13, bf16[4,1024,128]{2,1,0:T(8,128)(2,1)} %bitcast.160), kind=kOutput, calls=%fused_computation.6 | convolution fusion | flops 1634725888 | bytes 28590080 | tf_op jit(solution)/shard_map/rkgd,kld->kgrl/dot_general | solution.py:72
  89.5 11.0 %fusion.32 = bf16[512,4,2,128]{0,3,2,1:T(8,128)(2,1)S(1)} fusion(f32[4,1536,512,2]{2,1,3,0:T(8,128)} %get-tuple-element.20, pred[512,1536]{0,1:T(8,128)(4,1)S(1)} %copy-done.10, bf16[4,512,128]{1,2,0:T(8,128)(2,1)S(1)} %fusion.57, bf16[4,1024,128]{1,2,0:T(8,128)(2,1)S(1)} %bitcast.146, f32[512,4,2]{0,2,1:T(2,128)S(1)} %bitcast.165), kind=kOutput, calls=%fused_computation.40 | convolution fusion | flops 1633681408 | bytes 28590080 | tf_op jit(solution)/shard_map/kgrl,kld->kgrd/dot_general | solution.py:78
  100.6 4.7 %fusion.16 = bf16[512,2688]{1,0:T(8,128)(2,1)} fusion(bf16[512,1024]{0,1:T(8,128)(2,1)S(1)} %bitcast.163, bf16[1,1024,2688]{2,1,0:T(8,128)(2,1)S(1)} %bitcast.159), kind=kOutput, calls=%fused_computation.20 | convolution fusion | flops 2819948544 | bytes 9306112 | tf_op jit(solution)/shard_map/dot_general | solution.py:151
  105.3 0.0 reduce-scatter.5.cloned.1.call-start
  105.4 0.6 copy-done.19
  106.0 40.6 %reduce-scatter.3.cloned.1.call-done = bf16[128,2688]{1,0:T(8,128)(2,1)} async-done(((bf16[512,2688]{1,0:T(8,128)(2,1)}), bf16[128,2688]{1,0:T(8,128)(2,1)}) %reduce-scatter.3.cloned.1.call-update) | async-done | bytes 688144 | tf_op jit(solution)/shard_map/reduce_scatter | solution.py:150
  146.6 1.3 fusion.42
  147.9 1.4 fusion.45
  149.4 1.6 collective-permute-start.3
  151.0 1.7 collective-permute-done.3
  152.7 0.1 bitcast_select_fusion.2
  152.8 1.5 collective-permute-start.4
  154.3 1.5 collective-permute-start.6
  155.8 9.2 %collective-permute-done.4 = bf16[128,2688]{1,0:T(8,128)(2,1)S(1)} collective-permute-done((bf16[128,2688]{1,0:T(8,128)(2,1)S(1)}, bf16[128,2688]{1,0:T(8,128)(2,1)S(1)}, u32[]{:S(2)}, u32[]{:S(2)}) %collective-permute-start.4) | collective-permute-done | bytes 688160 | tf_op jit(solution)/shard_map/ppermute | solution.py:128
  165.0 0.6 collective-permute-start.5
  165.6 2.5 and_and_fusion
  168.1 11.7 %collective-permute-done.6 = bf16[128,2688]{1,0:T(8,128)(2,1)S(1)} collective-permute-done((bf16[128,2688]{1,0:T(8,128)(2,1)S(1)}, bf16[128,2688]{1,0:T(8,128)(2,1)S(1)}, u32[]{:S(2)}, u32[]{:S(2)}) %collective-permute-start.6) | collective-permute-done | bytes 688160 | tf_op jit(solution)/shard_map/ppermute | solution.py:131
  179.7 14.7 %collective-permute-done.5 = bf16[128,2688]{1,0:T(8,128)(2,1)S(1)} collective-permute-done((bf16[128,2688]{1,0:T(8,128)(2,1)S(1)}, bf16[128,2688]{1,0:T(8,128)(2,1)S(1)}, u32[]{:S(2)}, u32[]{:S(2)}) %collective-permute-start.5) | collective-permute-done | bytes 688160 | tf_op jit(solution)/shard_map/ppermute | solution.py:128
  194.5 1.4 pad_maximum_fusion.1
  195.9 2.4 gather_fusion.1
  198.3 2.2 multiply_convert_fusion
  200.5 8.9 %fusion.74 = f32[512,4,4,128]{0,3,2,1:T(8,128)S(1)} fusion(bf16[512,2688,1,1]{1,0,3,2:T(8,128)(2,1)S(1)} %bitcast.141, bf16[4,4,128,2688]{3,2,1,0:T(8,128)(2,1)} %bitcast.139), kind=kOutput, calls=%fused_computation.130 | convolution fusion | flops 5637144576 | bytes 17956864 | tf_op jit(solution)/shard_map/dot_general | solution.py:140
  209.5 0.1 multiply_reduce_fusion.2
  209.6 0.3 multiply_reduce_fusion
  209.9 0.9 fusion.58
  210.8 0.1 multiply_multiply_fusion.2
  211.0 0.5 multiply_multiply_fusion
  211.4 0.3 copy-done.3
  211.7 0.1 copy-done.4
  211.8 1.4 subtract_convert_fusion
  213.1 0.2 subtract_convert_fusion.2
  213.4 1.0 copy.19
  214.4 16.7 %fusion = (f32[4,2,512]{2,1,0:T(2,128)S(1)}, f32[4,2048,512,2]{2,1,3,0:T(8,128)}) fusion(pred[512,2048]{0,1:T(8,128)(4,1)S(1)} %copy-done.9, bf16[512,4,2,64]{0,3,2,1:T(8,128)(2,1)} %get-tuple-element.6, bf16[512,4,2,64]{0,3,2,1:T(8,128)(2,1)} %get-tuple-element.5, bf16[4,512,128]{2,1,0:T(8,128)(2,1)} %copy.19, bf16[4,512,128]{2,1,0:T(8,128)(2,1)} %copy-done.17, ...), kind=kOutput, calls=%fused_computation.3 | convolution fusion | flops 2181033984 | bytes 37765120 | tf_op jit(solution)/shard_map/rkgd,kld->kgrl/dot_general | solution.py:72
  231.1 15.1 %fusion.31 = bf16[512,4,2,128]{0,3,2,1:T(8,128)(2,1)} fusion(f32[4,2048,512,2]{2,1,3,0:T(8,128)} %get-tuple-element.22, pred[512,2048]{0,1:T(8,128)(4,1)S(1)} %copy-done.9, bf16[4,512,128]{1,2,0:T(8,128)(2,1)} %fusion.58, bf16[4,512,128]{1,2,0:T(8,128)(2,1)S(1)} %copy-done.16, bf16[4,1024,128]{1,2,0:T(8,128)(2,1)S(1)} %bitcast.147, ...), kind=kOutput, calls=%fused_computation.38 | convolution fusion | flops 2179989504 | bytes 37765120 | tf_op jit(solution)/shard_map/kgrl,kld->kgrd/dot_general | solution.py:78
  246.3 7.6 %fusion.19 = bf16[512,2688]{1,0:T(8,128)(2,1)} fusion(bf16[512,1024]{0,1:T(8,128)(2,1)} %bitcast.162, bf16[1,1024,2688]{2,1,0:T(8,128)(2,1)} %param.20), kind=kOutput, calls=%fused_computation.21 | convolution fusion | flops 2819948544 | bytes 9306112 | tf_op jit(solution)/shard_map/dot_general | solution.py:151
  253.9 54.0 %reduce-scatter.5.cloned.1.call-done = bf16[128,2688]{1,0:T(8,128)(2,1)} async-done(((bf16[512,2688]{1,0:T(8,128)(2,1)}), bf16[128,2688]{1,0:T(8,128)(2,1)}) %reduce-scatter.5.cloned.1.call-update) | async-done | bytes 688144 | tf_op jit(solution)/shard_map/reduce_scatter | solution.py:150
  307.9 1.3 fusion.46
  309.3 1.4 fusion.56
  310.7 1.2 maximum_bitcast_fusion.10
  (68 shorter events, 0.4 us)
Async XLA Ops:
  6.5 140.1 %reduce-scatter.3.cloned.1.call-start = ((), (), s32[]{:S(2)}) async-start(), calls=%async_computation.2 | async-start | bytes 3440640 | tf_op jit(solution)/shard_map/reduce_scatter | solution.py:150
  6.5 33.2 %collective-permute-start = (bf16[128,2688]{1,0:T(8,128)(2,1)}, bf16[128,2688]{1,0:T(8,128)(2,1)S(1)}, u32[]{:S(2)}, u32[]{:S(2)}) collective-permute-start(bf16[128,2688]{1,0:T(8,128)(2,1)} %bitcast.144), channel_id=1, source_target_pairs={{0,1},{1,2},{2,3},{3,0},{4,5},{5,6},{6,7},{7,4},{8,9},{9,10},{10,1... | collective-permute-start | bytes 2064392 | tf_op jit(solution)/shard_map/ppermute | solution.py:128
  9.5 35.2 %collective-permute-start.2 = (bf16[128,2688]{1,0:T(8,128)(2,1)}, bf16[128,2688]{1,0:T(8,128)(2,1)S(1)}, u32[]{:S(2)}, u32[]{:S(2)}) collective-permute-start(bf16[128,2688]{1,0:T(8,128)(2,1)} %bitcast.145), channel_id=1, source_target_pairs={{1,0},{2,1},{3,2},{0,3},{5,4},{6,5},{7,6},{4,7},{9,8},{10,9},{11,1... | collective-permute-start | bytes 2064392 | tf_op jit(solution)/shard_map/ppermute | solution.py:131
  25.5 14.1 %copy-start.18 = (f32[1,2688]{1,0:T(1,128)S(1)}, f32[1,2688]{1,0:T(1,128)}, u32[]{:S(2)}) copy-start(f32[1,2688]{1,0:T(1,128)} %param.14) | copy-start | bytes 32260
  25.5 32.3 %copy-start.2 = (bf16[1,128,2688]{2,1,0:T(8,128)(2,1)S(1)}, bf16[1,128,2688]{2,1,0:T(8,128)(2,1)}, u32[]{:S(2)}) copy-start(bf16[1,128,2688]{2,1,0:T(8,128)(2,1)} %param.11) | copy-start | bytes 2064388
  39.8 18.0 %copy-start.12 = (bf16[128,2688]{1,0:T(8,128)(2,1)}, bf16[128,2688]{1,0:T(8,128)(2,1)S(1)}, u32[]{:S(2)}) copy-start(bf16[128,2688]{1,0:T(8,128)(2,1)S(1)} %collective-permute-done) | copy-start | bytes 2064388
  39.8 18.0 %collective-permute-start.1 = (bf16[128,2688]{1,0:T(8,128)(2,1)S(1)}, bf16[128,2688]{1,0:T(8,128)(2,1)S(1)}, u32[]{:S(2)}, u32[]{:S(2)}) collective-permute-start(bf16[128,2688]{1,0:T(8,128)(2,1)S(1)} %collective-permute-done), channel_id=1, source_target_pairs={{0,1},{1,2},{2,3},{3,0},{4,5},{5,6},{6,7},{7,4},{8,9},{9,10},{10,1... | collective-permute-start | bytes 2064392 | tf_op jit(solution)/shard_map/ppermute | solution.py:128
  44.7 13.1 %copy-start.13 = (bf16[128,2688]{1,0:T(8,128)(2,1)}, bf16[128,2688]{1,0:T(8,128)(2,1)S(1)}, u32[]{:S(2)}) copy-start(bf16[128,2688]{1,0:T(8,128)(2,1)S(1)} %collective-permute-done.2) | copy-start | bytes 2064388
  72.9 0.7 copy-start.20
  73.0 0.7 copy-start.21
  73.4 16.1 %copy-start.15 = (bf16[4,512,128]{1,2,0:T(8,128)(2,1)}, bf16[4,512,128]{1,2,0:T(8,128)(2,1)S(1)}, u32[]{:S(2)}) copy-start(bf16[4,512,128]{1,2,0:T(8,128)(2,1)S(1)} %fusion.57) | copy-start | bytes 1572868
  73.6 0.9 copy-start.5
  73.6 1.0 copy-start.6
  75.9 1.1 copy-start.10
  76.4 13.1 %copy-start.17 = (bf16[4,512,128]{2,1,0:T(8,128)(2,1)}, bf16[4,512,128]{2,1,0:T(8,128)(2,1)S(1)}, u32[]{:S(2)}) copy-start(bf16[4,512,128]{2,1,0:T(8,128)(2,1)S(1)} %copy.13) | copy-start | bytes 1572868
  77.0 12.5 %copy-start.7 = (bf16[1,4,1024,128]{2,3,1,0:T(8,128)(2,1)S(1)}, bf16[1,4,1024,128]{2,3,1,0:T(8,128)(2,1)}, u32[]{:S(2)}) copy-start(bf16[1,4,1024,128]{2,3,1,0:T(8,128)(2,1)} %copy.15) | copy-start | bytes 3145732
  77.0 23.5 %slice-start = ((s8[5505024]{0:T(1024)(128)(4,1)}), s8[4194304]{0:T(1024)(128)(4,1)S(1)}, s32[]{:S(2)}) async-start(s8[5505024]{0:T(1024)(128)(4,1)} %bitcast.158), calls=%async_computation.4 | async-start | bytes 8388608
  89.5 11.0 %slice-start.1 = ((s8[5505024]{0:T(1024)(128)(4,1)}), s8[1310720]{0:T(1024)(128)(4,1)S(1)}, s32[]{:S(2)}) async-start(s8[5505024]{0:T(1024)(128)(4,1)} %bitcast.158), calls=%async_computation.5 | async-start | bytes 2621440
  105.3 0.7 copy-start.19
  105.3 47.4 %copy-start.11 = (bf16[1,128,2688]{2,1,0:T(8,128)(2,1)S(1)}, bf16[1,128,2688]{2,1,0:T(8,128)(2,1)}, u32[]{:S(2)}) copy-start(bf16[1,128,2688]{2,1,0:T(8,128)(2,1)} %param.12) | copy-start | bytes 2064388
  105.3 202.6 %reduce-scatter.5.cloned.1.call-start = ((), (), s32[]{:S(2)}) async-start(), calls=%async_computation.3 | async-start | bytes 3440640 | tf_op jit(solution)/shard_map/reduce_scatter | solution.py:150
  149.4 45.1 %copy-start = (bf16[128,2688]{1,0:T(8,128)(2,1)}, bf16[128,2688]{1,0:T(8,128)(2,1)S(1)}, u32[]{:S(2)}) copy-start(bf16[128,2688]{1,0:T(8,128)(2,1)S(1)} %fusion.45) | copy-start | bytes 2064388
  149.4 3.3 %collective-permute-start.3 = (bf16[128,2688]{1,0:T(8,128)(2,1)S(1)}, bf16[128,2688]{1,0:T(8,128)(2,1)S(1)}, u32[]{:S(2)}, u32[]{:S(2)}) collective-permute-start(bf16[128,2688]{1,0:T(8,128)(2,1)S(1)} %fusion.45), channel_id=1, source_target_pairs={{0,4},{4,8},{8,12},{12,16},{16,20},{20,24},{24,28},{1,5},{5,9},{9,... | collective-permute-start | bytes 2064392 | tf_op jit(solution)/shard_map/ppermute | solution.py:26
  152.8 12.2 %collective-permute-start.4 = (bf16[128,2688]{1,0:T(8,128)(2,1)S(1)}, bf16[128,2688]{1,0:T(8,128)(2,1)S(1)}, u32[]{:S(2)}, u32[]{:S(2)}) collective-permute-start(bf16[128,2688]{1,0:T(8,128)(2,1)S(1)} %bitcast_select_fusion.2), channel_id=1, source_target_pairs={{0,1},{1,2},{2,3},{3,0},{4,5},{5,6},{6,7},{7,4},{8,9},{9,10},{10,1... | collective-permute-start | bytes 2064392 | tf_op jit(solution)/shard_map/ppermute | solution.py:128
  154.3 25.4 %collective-permute-start.6 = (bf16[128,2688]{1,0:T(8,128)(2,1)S(1)}, bf16[128,2688]{1,0:T(8,128)(2,1)S(1)}, u32[]{:S(2)}, u32[]{:S(2)}) collective-permute-start(bf16[128,2688]{1,0:T(8,128)(2,1)S(1)} %bitcast_select_fusion.2), channel_id=1, source_target_pairs={{1,0},{2,1},{3,2},{0,3},{5,4},{6,5},{7,6},{4,7},{9,8},{10,9},{11,1... | collective-permute-start | bytes 2064392 | tf_op jit(solution)/shard_map/ppermute | solution.py:131
  165.0 29.5 %copy-start.14 = (bf16[128,2688]{1,0:T(8,128)(2,1)}, bf16[128,2688]{1,0:T(8,128)(2,1)S(1)}, u32[]{:S(2)}) copy-start(bf16[128,2688]{1,0:T(8,128)(2,1)S(1)} %collective-permute-done.4) | copy-start | bytes 2064388
  165.0 29.5 %collective-permute-start.5 = (bf16[128,2688]{1,0:T(8,128)(2,1)S(1)}, bf16[128,2688]{1,0:T(8,128)(2,1)S(1)}, u32[]{:S(2)}, u32[]{:S(2)}) collective-permute-start(bf16[128,2688]{1,0:T(8,128)(2,1)S(1)} %collective-permute-done.4), channel_id=1, source_target_pairs={{0,1},{1,2},{2,3},{3,0},{4,5},{5,6},{6,7},{7,4},{8,9},{9,10},{10,1... | collective-permute-start | bytes 2064392 | tf_op jit(solution)/shard_map/ppermute | solution.py:128
  210.8 0.9 copy-start.3
  210.8 1.0 copy-start.4
  213.1 1.2 copy-start.9
  214.4 16.8 %copy-start.8 = (bf16[1,4,1024,128]{2,3,1,0:T(8,128)(2,1)S(1)}, bf16[1,4,1024,128]{2,3,1,0:T(8,128)(2,1)}, u32[]{:S(2)}) copy-start(bf16[1,4,1024,128]{2,3,1,0:T(8,128)(2,1)} %copy.15) | copy-start | bytes 3145732
  214.4 16.8 %copy-start.16 = (bf16[4,512,128]{1,2,0:T(8,128)(2,1)S(1)}, bf16[4,512,128]{1,2,0:T(8,128)(2,1)}, u32[]{:S(2)}) copy-start(bf16[4,512,128]{1,2,0:T(8,128)(2,1)} %copy-done.15) | copy-start | bytes 1572868
  253.9 56.8 %copy-start.1 = (bf16[128,2688]{1,0:T(8,128)(2,1)S(1)}, bf16[128,2688]{1,0:T(8,128)(2,1)}, u32[]{:S(2)}) copy-start(bf16[128,2688]{1,0:T(8,128)(2,1)} %copy-done) | copy-start | bytes 2064388
Sparse Core Ops, SparseCore 0:
  105.4 41.1 reduce-scatter.2
  254.0 53.8 reduce-scatter.4
